TPU v7x, 32 devices: a whole 2x2x4 slice. The times are simulated.
32 devices in a mesh: replica: 8 (over z, core), group: 4 (over y, x).
Axes of the slice: x: 2, y: 2, z: 4, core: 2. Of those that a mesh axis runs over, the one named last changes fastest.
Arguments:
- tokens: bfloat16 [4096, 2048], P(('replica', 'group')), may hold values from -6 to 6
- lengths: int32 [8], P('replica'), may hold values from 128 to 512, as said below
- exit_layers: int32 [4096], P(('replica', 'group')), may hold values from 7 to 20, as said below
- pre_gain: bfloat16 [2048], P('group'), may hold values from 0.099609375 to 1.8984375
- pre_shift: bfloat16 [2048], P('group'), may hold values from -3 to 3
- query_weight: bfloat16 [2048, 2048], P('group'), may hold values from -0.1875 to 0.1875
- query_bias: bfloat16 [2048], P('group'), may hold values from -3 to 3
- key_weight: bfloat16 [2048, 2048], P('group'), may hold values from -0.1875 to 0.1875
- value_weight: bfloat16 [2048, 2048], P('group'), may hold values from -0.125 to 0.125
- value_bias: bfloat16 [2048], P('group'), may hold values from -3 to 3
- out_weight: bfloat16 [2048, 2048], P('group'), may hold values from -0.5 to 0.5
- out_bias: bfloat16 [2048], P('group'), may hold values from -1.75 to 1.75
- mid_gain: bfloat16 [2048], P('group'), may hold values from 0.099609375 to 1.8984375
- mid_shift: bfloat16 [2048], P('group'), may hold values from -3 to 3
- up_weight: bfloat16 [2048, 8192], P(None, 'group'), may hold values from -0.125 to 0.125
- up_bias: bfloat16 [8192], P('group'), may hold values from -3 to 3
- down_weight: bfloat16 [8192, 2048], P('group'), may hold values from -0.0625 to 0.0625
- down_bias: bfloat16 [2048], P('group'), may hold values from -1.75 to 1.75
- cotangent: bfloat16 [4096, 2048], P(('replica', 'group')), may hold values from -6 to 6
Outputs:
- output: bfloat16 [4096, 2048], P(('replica', 'group'))
- token_grad: bfloat16 [4096, 2048], P(('replica', 'group'))
- pre_gain_grad: float32 [2048], P('group')
- pre_shift_grad: float32 [2048], P('group')
- query_weight_grad: float32 [2048, 2048], P('group')
- query_bias_grad: float32 [2048], P('group')
- key_weight_grad: float32 [2048, 2048], P('group')
- value_weight_grad: float32 [2048, 2048], P('group')
- value_bias_grad: float32 [2048], P('group')
- out_weight_grad: float32 [2048, 2048], P('group')
- out_bias_grad: float32 [2048], P('group')
- mid_gain_grad: float32 [2048], P('group')
- mid_shift_grad: float32 [2048], P('group')
- up_weight_grad: float32 [2048, 8192], P(None, 'group')
- up_bias_grad: float32 [8192], P('group')
- down_weight_grad: float32 [8192, 2048], P('group')
- down_bias_grad: float32 [2048], P('group')
Inputs may be any that keep to these rules, and one draw needn't show every extreme that they name: `lengths`: some sequence has length 512 and some other has length 128. Within each sequence, exit_layers never rise from one position to the next.
All inputs are finite; a program needn't handle non-finite values.
Results may differ from a plain program's by a relative error of at most 0.02.
Values may be sent and summed in bfloat16 or wider, within the bound.
No kernel may reach another device: no remote copies, remote signals or barrier semaphores. Data moves between devices by JAX's collectives and lax.ppermute only.
A program may use at most 640 MiB of HBM per device.

v0:
```python
import jax
import jax.numpy as jnp
from jax import lax
from jax.sharding import PartitionSpec as P

D = 2048
H = 32
HD = 64
LAYER = 12


def layer_norm(values):
    center = values - jnp.mean(values, -1, keepdims=True)
    spread = jnp.mean(center * center, -1, keepdims=True)
    factor = lax.rsqrt(spread + 1e-05)
    return (center * factor, factor)


def norm_back(grad, normal, factor):
    return factor * (
        grad
        - jnp.mean(grad, -1, keepdims=True)
        - normal * jnp.mean(grad * normal, -1, keepdims=True)
    )


def gelu(values):
    return (
        0.5
        * values
        * (1.0 + jnp.tanh(0.7978845608 * (values + 0.044715 * values * values * values)))
    )


def gelu_back(values, grad):
    inner = 0.7978845608 * (values + 0.044715 * values * values * values)
    tangent = jnp.tanh(inner)
    slope = 0.5 * (1.0 + tangent) + 0.5 * values * (1.0 - tangent * tangent) * 0.7978845608 * (
        1.0 + 3.0 * 0.044715 * values * values
    )
    return grad * slope


def split_heads(matrix):
    groups = max(1, H // 8)
    return matrix.reshape(matrix.shape[0], groups, H // groups, HD).transpose(1, 0, 2, 3)


def join_heads(heads):
    return heads.transpose(1, 0, 2, 3).reshape(heads.shape[1], D)


def score_block(query_group, key_group, allowed):
    scores = (
        jnp.einsum("qhd,khd->hqk", query_group, key_group, preferred_element_type=jnp.float32)
        * 0.125
    )
    return jnp.where(allowed[None], scores, -1e30)


def matmul(left, right):
    return jnp.dot(left, right, preferred_element_type=jnp.float32)


def column_sums(matrix):
    return jnp.sum(matrix.astype(jnp.float32), 0)


def shards(
    tokens,
    lengths,
    exit_layers,
    pre_gain,
    pre_shift,
    query_weight,
    query_bias,
    key_weight,
    value_weight,
    value_bias,
    out_weight,
    out_bias,
    mid_gain,
    mid_shift,
    up_weight,
    up_bias,
    down_weight,
    down_bias,
    cotangent,
):
    local_rows = tokens.shape[0]
    group_count = lax.axis_size("group")
    seq_rows = local_rows * group_count
    member = lax.axis_index("group")
    position = member * local_rows + jnp.arange(local_rows, dtype=jnp.int32)
    active = ((position < lengths[0]) & (exit_layers > LAYER)).astype(jnp.float32)[:, None]
    allowed = jnp.arange(seq_rows, dtype=jnp.int32)[None, :] <= position[:, None]
    (
        gain_one,
        shift_one,
        gain_two,
        shift_two,
        query_full,
        key_full,
        value_full,
        out_full,
        qbias_full,
        vbias_full,
        obias_full,
    ) = (
        lax.all_gather(pre_gain, "group", axis=0, tiled=True),
        lax.all_gather(pre_shift, "group", axis=0, tiled=True),
        lax.all_gather(mid_gain, "group", axis=0, tiled=True),
        lax.all_gather(mid_shift, "group", axis=0, tiled=True),
        lax.all_gather(query_weight, "group", axis=0, tiled=True),
        lax.all_gather(key_weight, "group", axis=0, tiled=True),
        lax.all_gather(value_weight, "group", axis=0, tiled=True),
        lax.all_gather(out_weight, "group", axis=0, tiled=True),
        lax.all_gather(query_bias, "group", axis=0, tiled=True),
        lax.all_gather(value_bias, "group", axis=0, tiled=True),
        lax.all_gather(out_bias, "group", axis=0, tiled=True),
    )
    inputs = tokens.astype(jnp.float32)
    normed_one, factor_one = layer_norm(inputs)
    attn_in = (normed_one * gain_one.astype(jnp.float32) + shift_one.astype(jnp.float32)).astype(
        jnp.bfloat16
    )
    queries = (matmul(attn_in, query_full) + qbias_full.astype(jnp.float32)).astype(jnp.bfloat16)
    keys_local = matmul(attn_in, key_full).astype(jnp.bfloat16)
    values_local = (matmul(attn_in, value_full) + vbias_full.astype(jnp.float32)).astype(
        jnp.bfloat16
    )
    keys_all, values_all = (
        lax.all_gather(keys_local, "group", axis=0, tiled=True),
        lax.all_gather(values_local, "group", axis=0, tiled=True),
    )
    query_heads = split_heads(queries)
    key_heads = split_heads(keys_all)
    value_heads = split_heads(values_all)

    def forward_group(operands):
        query_group, key_group, value_group = operands
        scores = score_block(query_group, key_group, allowed)
        top = jnp.max(scores, -1, keepdims=True)
        logsum = top + jnp.log(jnp.sum(jnp.exp(scores - top), -1, keepdims=True))
        weights = jnp.exp(scores - logsum).astype(jnp.bfloat16)
        context_part = jnp.einsum(
            "hqk,khd->qhd", weights, value_group, preferred_element_type=jnp.float32
        )
        return (context_part, logsum[..., 0])

    context_heads, logsums = lax.map(forward_group, (query_heads, key_heads, value_heads))
    context_low = join_heads(context_heads).astype(jnp.bfloat16)
    attn_out = matmul(context_low, out_full) + obias_full.astype(jnp.float32)
    hidden = inputs + active * attn_out
    normed_two, factor_two = layer_norm(hidden)
    ffn_in = (normed_two * gain_two.astype(jnp.float32) + shift_two.astype(jnp.float32)).astype(
        jnp.bfloat16
    )
    up_full, upbias_full, down_full, downbias_full = (
        lax.all_gather(up_weight, "group", axis=1, tiled=True),
        lax.all_gather(up_bias, "group", axis=0, tiled=True),
        lax.all_gather(down_weight, "group", axis=0, tiled=True),
        lax.all_gather(down_bias, "group", axis=0, tiled=True),
    )
    pre_act = matmul(ffn_in, up_full) + upbias_full.astype(jnp.float32)
    act_low = gelu(pre_act).astype(jnp.bfloat16)
    branch = matmul(act_low, down_full) + downbias_full.astype(jnp.float32)
    output = (hidden + active * branch).astype(jnp.bfloat16)
    first_gain, second_gain, query_back, key_back, value_back, out_back = (
        lax.all_gather(pre_gain, "group", axis=0, tiled=True),
        lax.all_gather(mid_gain, "group", axis=0, tiled=True),
        lax.all_gather(query_weight, "group", axis=0, tiled=True),
        lax.all_gather(key_weight, "group", axis=0, tiled=True),
        lax.all_gather(value_weight, "group", axis=0, tiled=True),
        lax.all_gather(out_weight, "group", axis=0, tiled=True),
    )
    grad_out = cotangent.astype(jnp.float32)
    branch_grad = (active * grad_out).astype(jnp.bfloat16)
    up_back, down_back = (
        lax.all_gather(up_weight, "group", axis=1, tiled=True),
        lax.all_gather(down_weight, "group", axis=0, tiled=True),
    )
    act_grad = matmul(branch_grad, down_back.T)
    pre_grad = gelu_back(pre_act, act_grad).astype(jnp.bfloat16)
    ffn_in_grad = matmul(pre_grad, up_back.T)
    up_grad, up_bias_grad, down_grad, down_bias_grad = (
        lax.psum_scatter(
            matmul(ffn_in.T, pre_grad).astype(jnp.bfloat16),
            "group",
            scatter_dimension=1,
            tiled=True,
        ).astype(jnp.float32),
        lax.psum_scatter(
            column_sums(pre_grad).astype(jnp.bfloat16), "group", scatter_dimension=0, tiled=True
        ).astype(jnp.float32),
        lax.psum_scatter(
            matmul(act_low.T, branch_grad).astype(jnp.bfloat16),
            "group",
            scatter_dimension=0,
            tiled=True,
        ).astype(jnp.float32),
        lax.psum_scatter(
            column_sums(branch_grad).astype(jnp.bfloat16), "group", scatter_dimension=0, tiled=True
        ).astype(jnp.float32),
    )
    mid_gain_part = jnp.sum(ffn_in_grad * normed_two, 0)
    mid_shift_part = jnp.sum(ffn_in_grad, 0)
    hidden_grad = grad_out + norm_back(
        ffn_in_grad * second_gain.astype(jnp.float32), normed_two, factor_two
    )
    attn_grad = (active * hidden_grad).astype(jnp.bfloat16)
    context_grad = matmul(attn_grad, out_back.T).astype(jnp.bfloat16)
    out_bias_part = column_sums(attn_grad)

    def backward_group(operands):
        query_group, key_group, value_group, grad_group, logsum_group = operands
        scores = score_block(query_group, key_group, allowed)
        probs = jnp.exp(scores - logsum_group[..., None])
        probs_grad = jnp.einsum(
            "qhd,khd->hqk", grad_group, value_group, preferred_element_type=jnp.float32
        )
        delta = jnp.sum(probs * probs_grad, -1, keepdims=True)
        score_grad = (probs * (probs_grad - delta)).astype(jnp.bfloat16)
        query_part = (
            jnp.einsum("hqk,khd->qhd", score_grad, key_group, preferred_element_type=jnp.float32)
            * 0.125
        )
        key_part = (
            jnp.einsum("hqk,qhd->khd", score_grad, query_group, preferred_element_type=jnp.float32)
            * 0.125
        )
        value_part = jnp.einsum(
            "hqk,qhd->khd",
            probs.astype(jnp.bfloat16),
            grad_group,
            preferred_element_type=jnp.float32,
        )
        return (query_part, key_part, value_part)

    query_parts, key_parts, value_parts = lax.map(
        backward_group, (query_heads, key_heads, value_heads, split_heads(context_grad), logsums)
    )
    query_grad = join_heads(query_parts).astype(jnp.bfloat16)
    key_sum, value_sum = (
        lax.psum_scatter(
            join_heads(key_parts).astype(jnp.bfloat16), "group", scatter_dimension=0, tiled=True
        ).astype(jnp.float32),
        lax.psum_scatter(
            join_heads(value_parts).astype(jnp.bfloat16), "group", scatter_dimension=0, tiled=True
        ).astype(jnp.float32),
    )
    key_grad = key_sum.astype(jnp.bfloat16)
    value_grad = value_sum.astype(jnp.bfloat16)
    in_grad = (
        matmul(query_grad, query_back.T)
        + matmul(key_grad, key_back.T)
        + matmul(value_grad, value_back.T)
    )
    pre_gain_part = jnp.sum(in_grad * normed_one, 0)
    pre_shift_part = jnp.sum(in_grad, 0)
    token_grad = (
        hidden_grad + norm_back(in_grad * first_gain.astype(jnp.float32), normed_one, factor_one)
    ).astype(jnp.bfloat16)
    (
        pre_gain_grad,
        pre_shift_grad,
        mid_gain_grad,
        mid_shift_grad,
        query_wgrad,
        key_wgrad,
        value_wgrad,
        out_wgrad,
        query_bgrad,
        value_bgrad,
        out_bgrad,
    ) = (
        lax.psum_scatter(
            pre_gain_part.astype(jnp.bfloat16), "group", scatter_dimension=0, tiled=True
        ).astype(jnp.float32),
        lax.psum_scatter(
            pre_shift_part.astype(jnp.bfloat16), "group", scatter_dimension=0, tiled=True
        ).astype(jnp.float32),
        lax.psum_scatter(
            mid_gain_part.astype(jnp.bfloat16), "group", scatter_dimension=0, tiled=True
        ).astype(jnp.float32),
        lax.psum_scatter(
            mid_shift_part.astype(jnp.bfloat16), "group", scatter_dimension=0, tiled=True
        ).astype(jnp.float32),
        lax.psum_scatter(
            matmul(attn_in.T, query_grad).astype(jnp.bfloat16),
            "group",
            scatter_dimension=0,
            tiled=True,
        ).astype(jnp.float32),
        lax.psum_scatter(
            matmul(attn_in.T, key_grad).astype(jnp.bfloat16),
            "group",
            scatter_dimension=0,
            tiled=True,
        ).astype(jnp.float32),
        lax.psum_scatter(
            matmul(attn_in.T, value_grad).astype(jnp.bfloat16),
            "group",
            scatter_dimension=0,
            tiled=True,
        ).astype(jnp.float32),
        lax.psum_scatter(
            matmul(context_low.T, attn_grad).astype(jnp.bfloat16),
            "group",
            scatter_dimension=0,
            tiled=True,
        ).astype(jnp.float32),
        lax.psum_scatter(
            column_sums(query_grad).astype(jnp.bfloat16), "group", scatter_dimension=0, tiled=True
        ).astype(jnp.float32),
        lax.psum_scatter(
            column_sums(value_grad).astype(jnp.bfloat16), "group", scatter_dimension=0, tiled=True
        ).astype(jnp.float32),
        lax.psum_scatter(
            out_bias_part.astype(jnp.bfloat16), "group", scatter_dimension=0, tiled=True
        ).astype(jnp.float32),
    )
    totals = (
        lax.psum(pre_gain_grad.astype(jnp.bfloat16), "replica").astype(jnp.float32),
        lax.psum(pre_shift_grad.astype(jnp.bfloat16), "replica").astype(jnp.float32),
        lax.psum(query_wgrad.astype(jnp.bfloat16), "replica").astype(jnp.float32),
        lax.psum(query_bgrad.astype(jnp.bfloat16), "replica").astype(jnp.float32),
        lax.psum(key_wgrad.astype(jnp.bfloat16), "replica").astype(jnp.float32),
        lax.psum(value_wgrad.astype(jnp.bfloat16), "replica").astype(jnp.float32),
        lax.psum(value_bgrad.astype(jnp.bfloat16), "replica").astype(jnp.float32),
        lax.psum(out_wgrad.astype(jnp.bfloat16), "replica").astype(jnp.float32),
        lax.psum(out_bgrad.astype(jnp.bfloat16), "replica").astype(jnp.float32),
        lax.psum(mid_gain_grad.astype(jnp.bfloat16), "replica").astype(jnp.float32),
        lax.psum(mid_shift_grad.astype(jnp.bfloat16), "replica").astype(jnp.float32),
        lax.psum(up_grad.astype(jnp.bfloat16), "replica").astype(jnp.float32),
        lax.psum(up_bias_grad.astype(jnp.bfloat16), "replica").astype(jnp.float32),
        lax.psum(down_grad.astype(jnp.bfloat16), "replica").astype(jnp.float32),
        lax.psum(down_bias_grad.astype(jnp.bfloat16), "replica").astype(jnp.float32),
    )
    return (
        output,
        token_grad,
        totals[0],
        totals[1],
        totals[2],
        totals[3],
        totals[4],
        totals[5],
        totals[6],
        totals[7],
        totals[8],
        totals[9],
        totals[10],
        totals[11],
        totals[12],
        totals[13],
        totals[14],
    )


def solution(mesh):
    return jax.shard_map(
        shards,
        mesh=mesh,
        in_specs=(
            P(("replica", "group"), None),
            P("replica"),
            P(("replica", "group")),
            P("group"),
            P("group"),
            P("group", None),
            P("group"),
            P("group", None),
            P("group", None),
            P("group"),
            P("group", None),
            P("group"),
            P("group"),
            P("group"),
            P(None, "group"),
            P("group"),
            P("group", None),
            P("group"),
            P(("replica", "group"), None),
        ),
        out_specs=(
            P(("replica", "group"), None),
            P(("replica", "group"), None),
            P("group"),
            P("group"),
            P("group", None),
            P("group"),
            P("group", None),
            P("group", None),
            P("group"),
            P("group", None),
            P("group"),
            P("group"),
            P("group"),
            P(None, "group"),
            P("group"),
            P("group", None),
            P("group"),
        ),
        check_vma=False,
    )
```

profile of v0, /device:TPU:0, one launch (start us, length us, event | category | flops | bytes accessed | tf_op | source)
XLA Modules:
  0.0 2687.4 jit_solution(7998907598796842740)
XLA Ops:
  34.8 65.6 %all-gather.17.cloned.1.call-done = bf16[2048,2048]{1,0:T(8,128)(2,1)} async-done(((bf16[512,2048]{1,0:T(8,128)(2,1)}), bf16[2048,2048]{1,0:T(8,128)(2,1)}) %all-gather.17.cloned.1.call-update) | async-done | bytes 8388624 | tf_op jit(solution)/shard_map/all_gather | solution.py:116
  105.9 83.9 %all-gather.23.cloned.1.call-done = bf16[2048,2048]{1,0:T(8,128)(2,1)} async-done(((bf16[512,2048]{1,0:T(8,128)(2,1)}), bf16[2048,2048]{1,0:T(8,128)(2,1)}) %all-gather.23.cloned.1.call-update) | async-done | bytes 8388624 | tf_op jit(solution)/shard_map/all_gather | solution.py:115
  237.1 42.5 %all-gather.21.cloned.1.call-done = bf16[2048,2048]{1,0:T(8,128)(2,1)} async-done(((bf16[512,2048]{1,0:T(8,128)(2,1)}), bf16[2048,2048]{1,0:T(8,128)(2,1)}) %all-gather.21.cloned.1.call-update) | async-done | bytes 8388624 | tf_op jit(solution)/shard_map/all_gather | solution.py:114
  284.6 32.6 %all-gather.19.cloned.1.call-done = bf16[512,2048]{1,0:T(8,128)(2,1)} async-done(((bf16[128,2048]{1,0:T(8,128)(2,1)}), bf16[512,2048]{1,0:T(8,128)(2,1)}) %all-gather.19.cloned.1.call-update) | async-done | bytes 2097168 | tf_op jit(solution)/shard_map/all_gather | solution.py:134
  321.3 33.5 %all-gather.25.cloned.1.call-done = bf16[512,2048]{1,0:T(8,128)(2,1)} async-done(((bf16[128,2048]{1,0:T(8,128)(2,1)}), bf16[512,2048]{1,0:T(8,128)(2,1)}) %all-gather.25.cloned.1.call-update) | async-done | bytes 2097168 | tf_op jit(solution)/shard_map/all_gather | solution.py:133
  374.4 69.8 %all-gather.27.cloned.1.call-done = bf16[2048,2048]{1,0:T(8,128)(2,1)} async-done(((bf16[512,2048]{1,0:T(8,128)(2,1)}), bf16[2048,2048]{1,0:T(8,128)(2,1)}) %all-gather.27.cloned.1.call-update) | async-done | bytes 8388624 | tf_op jit(solution)/shard_map/all_gather | solution.py:117
  450.3 292.9 %all-gather.29.cloned.1.call-done = bf16[2048,8192]{1,0:T(8,128)(2,1)} async-done(((bf16[2048,2048]{1,0:T(8,128)(2,1)}), bf16[2048,8192]{1,0:T(8,128)(2,1)}) %all-gather.29.cloned.1.call-update) | async-done | bytes 33554448 | tf_op jit(solution)/shard_map/all_gather | solution.py:160
  743.3 20.8 convolution_add_fusion
  764.0 278.3 %all-gather.31.cloned.1.call-done = bf16[8192,2048]{1,0:T(8,128)(2,1)} async-done(((bf16[2048,2048]{1,0:T(8,128)(2,1)}), bf16[8192,2048]{1,0:T(8,128)(2,1)}) %all-gather.31.cloned.1.call-update) | async-done | bytes 33554448 | tf_op jit(solution)/shard_map/all_gather | solution.py:162
  1042.3 18.8 fusion.81
  1061.2 19.7 multiply_reduce_fusion.1
  1095.0 31.3 %while.29 = (s32[]{:T(128)}, bf16[4,128,8,64]{1,3,2,0:T(8,128)(2,1)}, bf16[4,512,8,64]{1,3,2,0:T(8,128)(2,1)}, bf16[4,512,8,64]{1,3,2,0:T(8,128)(2,1)}, bf16[4,5...) while((s32[]{:T(128)}, ...), condition=%wide.region_12.13_spmd.clone, body=%wide.region_10.12_spmd.clone.sunk | while | flops 340655104 | bytes 58091296 | solution.py:240
  1147.0 18.6 reduce-scatter.25.cloned.1.call-done
  1172.5 31.9 %reduce-scatter.27.cloned.1.call-done = bf16[128,2048]{1,0:T(8,128)(2,1)} async-done(((bf16[512,2048]{1,0:T(8,128)(2,1)}), bf16[128,2048]{1,0:T(8,128)(2,1)}) %reduce-scatter.27.cloned.1.call-update) | async-done | bytes 524304
  1229.1 16.6 convolution_convert_fusion.1
  1245.8 48.8 %reduce-scatter.15.cloned.1.call-done = bf16[512,2048]{1,0:T(8,128)(2,1)} async-done(((bf16[2048,2048]{1,0:T(8,128)(2,1)}), bf16[512,2048]{1,0:T(8,128)(2,1)}) %reduce-scatter.15.cloned.1.call-update) | async-done | bytes 2097168 | tf_op jit(solution)/shard_map/reduce_scatter | solution.py:289
  1294.5 89.6 %reduce-scatter.21.cloned.1.call-done = bf16[512,2048]{1,0:T(8,128)(2,1)} async-done(((bf16[2048,2048]{1,0:T(8,128)(2,1)}), bf16[512,2048]{1,0:T(8,128)(2,1)}) %reduce-scatter.21.cloned.1.call-update) | async-done | bytes 2097168 | tf_op jit(solution)/shard_map/reduce_scatter | solution.py:307
  1384.2 90.1 %reduce-scatter.17.cloned.1.call-done = bf16[512,2048]{1,0:T(8,128)(2,1)} async-done(((bf16[2048,2048]{1,0:T(8,128)(2,1)}), bf16[512,2048]{1,0:T(8,128)(2,1)}) %reduce-scatter.17.cloned.1.call-update) | async-done | bytes 2097168 | tf_op jit(solution)/shard_map/reduce_scatter | solution.py:295
  1474.2 89.6 %reduce-scatter.19.cloned.1.call-done = bf16[512,2048]{1,0:T(8,128)(2,1)} async-done(((bf16[2048,2048]{1,0:T(8,128)(2,1)}), bf16[512,2048]{1,0:T(8,128)(2,1)}) %reduce-scatter.19.cloned.1.call-update) | async-done | bytes 2097168 | tf_op jit(solution)/shard_map/reduce_scatter | solution.py:301
  1563.9 291.6 %reduce-scatter.23.cloned.1.call-done = bf16[2048,2048]{1,0:T(8,128)(2,1)} async-done(((bf16[2048,8192]{1,0:T(8,128)(2,1)}), bf16[2048,2048]{1,0:T(8,128)(2,1)}) %reduce-scatter.23.cloned.1.call-update) | async-done | bytes 8388624 | tf_op jit(solution)/shard_map/reduce_scatter | solution.py:187
  1855.5 291.9 %reduce-scatter.29.cloned.1.call-done = bf16[2048,2048]{1,0:T(8,128)(2,1)} async-done(((bf16[8192,2048]{1,0:T(8,128)(2,1)}), bf16[2048,2048]{1,0:T(8,128)(2,1)}) %reduce-scatter.29.cloned.1.call-update) | async-done | bytes 8388624
  2164.9 18.0 fusion.52
  2213.1 28.0 %all-reduce.10 = (bf16[512]{0:T(512)(128)(2,1)S(1)}, bf16[512]{0:T(512)(128)(2,1)S(1)}, bf16[512]{0:T(512)(128)(2,1)S(1)}, bf16[512]{0:T(512)(128)(2,1)S(1)}, bf...) all-reduce(bf16[512]{0:T(512)(128)(2,1)S(1)} %dynamic-slice.1, ...), channel_id=1, replica_groups=mesh['replica'=8,'group'=4] {'replica'}, use_global_device_ids=true, to_apply=%region_19.20 | all-reduce | flops 6144 | bytes 24576 | tf_op jit(solution)/shard_map/psum | solution.py:324
  2247.6 397.6 %all-reduce.15.cloned.1.call-done = (bf16[512,2048]{1,0:T(8,128)(2,1)}, bf16[512,2048]{1,0:T(8,128)(2,1)}, bf16[512,2048]{1,0:T(8,128)(2,1)}, bf16[512,2048]{1,0...) async-done(((bf16[512,2048]{1,0:T(8,128)(2,1)}, bf16[512,2048]{1,0:T(8,128)(2,1)}, bf16[512,2048]{1,0:T(8,128)(2,1)}, bf16[512,2048]{1,0:T(8,128)(2,1)}, ...) | async-done | bytes 25165840 | tf_op jit(solution)/shard_map/psum | solution.py:326
  (292 shorter events, 315.1 us)
Async XLA Ops:
  7.2 19.9 copy-start.24
  7.2 27.1 %copy-start = (bf16[128,2048]{1,0:T(8,128)(2,1)S(1)}, bf16[128,2048]{1,0:T(8,128)(2,1)}, u32[]{:S(2)}) copy-start(bf16[128,2048]{1,0:T(8,128)(2,1)} %param.23) | copy-start | bytes 1572868
  7.2 93.1 %all-gather.17.cloned.1.call-start = ((), (), s32[]{:S(2)}) async-start(), calls=%async_computation.8 | async-start | bytes 10485760 | tf_op jit(solution)/shard_map/all_gather | solution.py:116
  8.0 181.9 %all-gather.23.cloned.1.call-start = ((), (), s32[]{:S(2)}) async-start(), calls=%async_computation.11 | async-start | bytes 10485760 | tf_op jit(solution)/shard_map/all_gather | solution.py:115
  8.7 270.9 %all-gather.21.cloned.1.call-start = ((), (), s32[]{:S(2)}) async-start(), calls=%async_computation.10 | async-start | bytes 10485760 | tf_op jit(solution)/shard_map/all_gather | solution.py:114
  9.4 307.7 %all-gather.19.cloned.1.call-start = ((), (), s32[]{:S(2)}) async-start(), calls=%async_computation.9 | async-start | bytes 2621440 | tf_op jit(solution)/shard_map/all_gather | solution.py:134
  105.9 248.9 %all-gather.25.cloned.1.call-start = ((), (), s32[]{:S(2)}) async-start(), calls=%async_computation.12 | async-start | bytes 2621440 | tf_op jit(solution)/shard_map/all_gather | solution.py:133
  195.4 248.8 %all-gather.27.cloned.1.call-start = ((), (), s32[]{:S(2)}) async-start(), calls=%async_computation.13 | async-start | bytes 10485760 | tf_op jit(solution)/shard_map/all_gather | solution.py:117
  195.9 547.3 %all-gather.29.cloned.1.call-start = ((), (), s32[]{:S(2)}) async-start(), calls=%async_computation.14 | async-start | bytes 41943040 | tf_op jit(solution)/shard_map/all_gather | solution.py:160
  196.7 25.1 copy-start.27
  196.7 32.2 %copy-start.28 = (bf16[512]{0:T(512)(128)(2,1)S(1)}, bf16[512]{0:T(512)(128)(2,1)}, u32[]{:S(2)}) copy-start(bf16[512]{0:T(512)(128)(2,1)} %param.35) | copy-start | bytes 3076
  196.7 40.3 %copy-start.30 = (s32[128]{0:T(128)S(1)}, s32[128]{0:T(128)}, u32[]{:S(2)}) copy-start(s32[128]{0:T(128)} %param.25) | copy-start | bytes 1540
  196.8 845.6 %all-gather.31.cloned.1.call-start = ((), (), s32[]{:S(2)}) async-start(), calls=%async_computation.15 | async-start | bytes 41943040 | tf_op jit(solution)/shard_map/all_gather | solution.py:162
  197.5 968.0 %reduce-scatter.25.cloned.1.call-start = ((), (), s32[]{:S(2)}) async-start(), calls=%async_computation.21 | async-start | bytes 2621440
  1130.2 74.2 %reduce-scatter.27.cloned.1.call-start = ((), (), s32[]{:S(2)}) async-start(), calls=%async_computation.22 | async-start | bytes 2621440
  1134.2 160.3 %reduce-scatter.15.cloned.1.call-start = ((), (), s32[]{:S(2)}) async-start(), calls=%async_computation.16 | async-start | bytes 10485760 | tf_op jit(solution)/shard_map/reduce_scatter | solution.py:289
  1140.2 244.0 %reduce-scatter.21.cloned.1.call-start = ((), (), s32[]{:S(2)}) async-start(), calls=%async_computation.19 | async-start | bytes 10485760 | tf_op jit(solution)/shard_map/reduce_scatter | solution.py:307
  1146.9 327.3 %reduce-scatter.17.cloned.1.call-start = ((), (), s32[]{:S(2)}) async-start(), calls=%async_computation.17 | async-start | bytes 10485760 | tf_op jit(solution)/shard_map/reduce_scatter | solution.py:295
  1172.5 391.4 %reduce-scatter.19.cloned.1.call-start = ((), (), s32[]{:S(2)}) async-start(), calls=%async_computation.18 | async-start | bytes 10485760 | tf_op jit(solution)/shard_map/reduce_scatter | solution.py:301
  1211.2 644.3 %reduce-scatter.23.cloned.1.call-start = ((), (), s32[]{:S(2)}) async-start(), calls=%async_computation.20 | async-start | bytes 41943040 | tf_op jit(solution)/shard_map/reduce_scatter | solution.py:187
  1228.1 919.2 %reduce-scatter.29.cloned.1.call-start = ((), (), s32[]{:S(2)}) async-start(), calls=%async_computation.23 | async-start | bytes 41943040
  1245.7 1399.5 %all-reduce.15.cloned.1.call-start = ((), (), s32[]{:S(2)}) async-start(), calls=%async_computation.24 | async-start | bytes 50331648 | tf_op jit(solution)/shard_map/psum | solution.py:326
  2164.8 18.1 copy-start.9
  2189.5 56.9 %copy-start.12 = (f32[128,2048]{1,0:T(8,128)S(1)}, f32[128,2048]{1,0:T(8,128)}, u32[]{:S(2)}) copy-start(f32[128,2048]{1,0:T(8,128)} %get-tuple-element.224) | copy-start | bytes 3145732
  (49 other events, 125.0 us)
Sparse Core Ops, SparseCore 0:
  9.9 90.3 all-gather.16
  102.2 87.5 all-gather.22
  191.7 87.8 all-gather.20
  281.8 35.3 all-gather.18
  319.5 35.2 all-gather.24
  356.5 87.5 all-gather.26
  446.0 297.2 all-gather.28
  745.1 297.2 all-gather.30
  1130.3 35.1 reduce-scatter.24
  1169.2 35.1 reduce-scatter.26
  1208.1 86.3 reduce-scatter.14
  1297.7 86.3 reduce-scatter.20
  1387.8 86.3 reduce-scatter.16
  1477.4 86.3 reduce-scatter.18
  1566.8 288.6 reduce-scatter.22
  1858.7 288.6 reduce-scatter.28
  2150.5 494.6 all-reduce.14
where the time goes:
time: 2690 us
  waiting for transfers between devices  2250 us (84%)
  matrix products  210 us (8%)
  blocking collectives  116 us (4%)
  other arithmetic  50.9 us (2%)
  local copies, waits for them, and re-layouts  39.5 us (1%)
    psum x1, waiting for transfers between devices, shards(): lax.psum(query_wgrad.astype(jnp.bfloat16), 'replica').astype(jnp.float32)  398 us
    unnamed x20, waiting for transfers between devices  346 us
    all_gather x1, waiting for transfers between devices, shards(): lax.all_gather(up_weight, 'group', axis=1, tiled=True)  293 us
    reduce_scatter x1, waiting for transfers between devices, shards(): lax.psum_scatter(matmul(ffn_in.T, pre_grad).astype(jnp.bfloat16), 'group'...  292 us
    all_gather x1, waiting for transfers between devices, shards(): lax.all_gather(down_weight, 'group', axis=0, tiled=True)  278 us
    dot_general x18, matrix products, matmul(): return jnp.dot(left, right, preferred_element_type=jnp.float32)  182 us
    reduce_scatter x1, waiting for transfers between devices, shards(): lax.psum_scatter(matmul(attn_in.T, key_grad).astype(jnp.bfloat16), 'group...  90.1 us
    reduce_scatter x1, waiting for transfers between devices, shards(): lax.psum_scatter(matmul(attn_in.T, value_grad).astype(jnp.bfloat16), 'gro...  89.6 us
  transfers between devices with their start and end apart: 17, of which 17 were waited for; matrix products, arithmetic and copies ran while one was open for 6% of the time, Pallas kernels for 0%

commit v1 on v0

--- a/solution.py
+++ b/solution.py
@@ -7,6 +7,11 @@
 H = 32
 HD = 64
 LAYER = 12
+
+
+def gather_and_add(x, mesh_axis):
+    parts = lax.all_gather(x, mesh_axis)
+    return jnp.sum(parts, axis=0)
 
 
 def layer_norm(values):
@@ -323,7 +328,7 @@
     totals = (
         lax.psum(pre_gain_grad.astype(jnp.bfloat16), "replica").astype(jnp.float32),
         lax.psum(pre_shift_grad.astype(jnp.bfloat16), "replica").astype(jnp.float32),
-        lax.psum(query_wgrad.astype(jnp.bfloat16), "replica").astype(jnp.float32),
+        gather_and_add(query_wgrad.astype(jnp.bfloat16), "replica").astype(jnp.float32),
         lax.psum(query_bgrad.astype(jnp.bfloat16), "replica").astype(jnp.float32),
         lax.psum(key_wgrad.astype(jnp.bfloat16), "replica").astype(jnp.float32),
         lax.psum(value_wgrad.astype(jnp.bfloat16), "replica").astype(jnp.float32),

time: 2690 us -> 2800 us (1.041)
  waiting for transfers between devices: 2250 us -> 2350 us
    all_gather x0 -> x1, waiting for transfers between devices: none -> 49.1 us  [gather_and_add(): parts = lax.all_gather(x, mesh_axis)]
    psum x1, waiting for transfers between devices: 398 us -> 443 us  [shards(): lax.psum(key_wgrad.astype(jnp.bfloat16), 'replica').astype(jnp.float32)]
    unnamed x20 -> x21, waiting for transfers between devices: 346 us -> 347 us
  transfers between devices with their start and end apart: 17 -> 18, of which waited for: 17 -> 18; matrix products, arithmetic and copies ran while one was open for 6% -> 7% of each run, Pallas kernels for 0% -> 0%
where the time goes in v1:
time: 2800 us
  waiting for transfers between devices  2350 us (84%)
  matrix products  212 us (8%)
  blocking collectives  118 us (4%)
  other arithmetic  60.7 us (2%)
  local copies, waits for them, and re-layouts  39.6 us (1%)
    psum x1, waiting for transfers between devices, shards(): lax.psum(key_wgrad.astype(jnp.bfloat16), 'replica').astype(jnp.float32)  443 us
    unnamed x21, waiting for transfers between devices  347 us
    all_gather x1, waiting for transfers between devices, shards(): lax.all_gather(up_weight, 'group', axis=1, tiled=True)  293 us
    reduce_scatter x1, waiting for transfers between devices, shards(): lax.psum_scatter(matmul(ffn_in.T, pre_grad).astype(jnp.bfloat16), 'group'...  292 us
    all_gather x1, waiting for transfers between devices, shards(): lax.all_gather(down_weight, 'group', axis=0, tiled=True)  278 us
    dot_general x18, matrix products, matmul(): return jnp.dot(left, right, preferred_element_type=jnp.float32)  183 us
    reduce_scatter x1, waiting for transfers between devices, shards(): lax.psum_scatter(matmul(attn_in.T, key_grad).astype(jnp.bfloat16), 'group...  90.1 us
    reduce_scatter x1, waiting for transfers between devices, shards(): lax.psum_scatter(matmul(attn_in.T, value_grad).astype(jnp.bfloat16), 'gro...  89.6 us
  transfers between devices with their start and end apart: 18, of which 18 were waited for; matrix products, arithmetic and copies ran while one was open for 7% of the time, Pallas kernels for 0%

profile of v1, /device:TPU:0, one launch (start us, length us, event | category | flops | bytes accessed | tf_op | source)
XLA Modules:
  0.0 2795.7 jit_solution(13291426279189481237)
XLA Ops:
  34.8 65.6 %all-gather.19.cloned.1.call-done = bf16[2048,2048]{1,0:T(8,128)(2,1)} async-done(((bf16[512,2048]{1,0:T(8,128)(2,1)}), bf16[2048,2048]{1,0:T(8,128)(2,1)}) %all-gather.19.cloned.1.call-update) | async-done | bytes 8388624 | tf_op jit(solution)/shard_map/all_gather | solution.py:121
  105.9 83.9 %all-gather.25.cloned.1.call-done = bf16[2048,2048]{1,0:T(8,128)(2,1)} async-done(((bf16[512,2048]{1,0:T(8,128)(2,1)}), bf16[2048,2048]{1,0:T(8,128)(2,1)}) %all-gather.25.cloned.1.call-update) | async-done | bytes 8388624 | tf_op jit(solution)/shard_map/all_gather | solution.py:120
  237.1 42.5 %all-gather.23.cloned.1.call-done = bf16[2048,2048]{1,0:T(8,128)(2,1)} async-done(((bf16[512,2048]{1,0:T(8,128)(2,1)}), bf16[2048,2048]{1,0:T(8,128)(2,1)}) %all-gather.23.cloned.1.call-update) | async-done | bytes 8388624 | tf_op jit(solution)/shard_map/all_gather | solution.py:119
  284.6 32.6 %all-gather.21.cloned.1.call-done = bf16[512,2048]{1,0:T(8,128)(2,1)} async-done(((bf16[128,2048]{1,0:T(8,128)(2,1)}), bf16[512,2048]{1,0:T(8,128)(2,1)}) %all-gather.21.cloned.1.call-update) | async-done | bytes 2097168 | tf_op jit(solution)/shard_map/all_gather | solution.py:139
  321.3 33.5 %all-gather.27.cloned.1.call-done = bf16[512,2048]{1,0:T(8,128)(2,1)} async-done(((bf16[128,2048]{1,0:T(8,128)(2,1)}), bf16[512,2048]{1,0:T(8,128)(2,1)}) %all-gather.27.cloned.1.call-update) | async-done | bytes 2097168 | tf_op jit(solution)/shard_map/all_gather | solution.py:138
  374.4 69.8 %all-gather.29.cloned.1.call-done = bf16[2048,2048]{1,0:T(8,128)(2,1)} async-done(((bf16[512,2048]{1,0:T(8,128)(2,1)}), bf16[2048,2048]{1,0:T(8,128)(2,1)}) %all-gather.29.cloned.1.call-update) | async-done | bytes 8388624 | tf_op jit(solution)/shard_map/all_gather | solution.py:122
  450.4 292.8 %all-gather.31.cloned.1.call-done = bf16[2048,8192]{1,0:T(8,128)(2,1)} async-done(((bf16[2048,2048]{1,0:T(8,128)(2,1)}), bf16[2048,8192]{1,0:T(8,128)(2,1)}) %all-gather.31.cloned.1.call-update) | async-done | bytes 33554448 | tf_op jit(solution)/shard_map/all_gather | solution.py:165
  743.3 20.8 convolution_add_fusion
  764.0 278.3 %all-gather.33.cloned.1.call-done = bf16[8192,2048]{1,0:T(8,128)(2,1)} async-done(((bf16[2048,2048]{1,0:T(8,128)(2,1)}), bf16[8192,2048]{1,0:T(8,128)(2,1)}) %all-gather.33.cloned.1.call-update) | async-done | bytes 33554448 | tf_op jit(solution)/shard_map/all_gather | solution.py:167
  1042.3 18.8 fusion.81
  1061.2 19.7 multiply_reduce_fusion.1
  1095.0 31.3 %while.29 = (s32[]{:T(128)}, bf16[4,128,8,64]{1,3,2,0:T(8,128)(2,1)}, bf16[4,512,8,64]{1,3,2,0:T(8,128)(2,1)}, bf16[4,512,8,64]{1,3,2,0:T(8,128)(2,1)}, bf16[4,5...) while((s32[]{:T(128)}, ...), condition=%wide.region_12.13_spmd.clone, body=%wide.region_10.12_spmd.clone.sunk | while | flops 340655104 | bytes 58091296 | solution.py:245
  1147.0 18.6 reduce-scatter.25.cloned.1.call-done
  1172.5 31.9 %reduce-scatter.27.cloned.1.call-done = bf16[128,2048]{1,0:T(8,128)(2,1)} async-done(((bf16[512,2048]{1,0:T(8,128)(2,1)}), bf16[128,2048]{1,0:T(8,128)(2,1)}) %reduce-scatter.27.cloned.1.call-update) | async-done | bytes 524304
  1245.7 48.8 %reduce-scatter.15.cloned.1.call-done = bf16[512,2048]{1,0:T(8,128)(2,1)} async-done(((bf16[2048,2048]{1,0:T(8,128)(2,1)}), bf16[512,2048]{1,0:T(8,128)(2,1)}) %reduce-scatter.15.cloned.1.call-update) | async-done | bytes 2097168 | tf_op jit(solution)/shard_map/reduce_scatter | solution.py:294
  1294.6 89.6 %reduce-scatter.21.cloned.1.call-done = bf16[512,2048]{1,0:T(8,128)(2,1)} async-done(((bf16[2048,2048]{1,0:T(8,128)(2,1)}), bf16[512,2048]{1,0:T(8,128)(2,1)}) %reduce-scatter.21.cloned.1.call-update) | async-done | bytes 2097168 | tf_op jit(solution)/shard_map/reduce_scatter | solution.py:312
  1384.1 90.1 %reduce-scatter.17.cloned.1.call-done = bf16[512,2048]{1,0:T(8,128)(2,1)} async-done(((bf16[2048,2048]{1,0:T(8,128)(2,1)}), bf16[512,2048]{1,0:T(8,128)(2,1)}) %reduce-scatter.17.cloned.1.call-update) | async-done | bytes 2097168 | tf_op jit(solution)/shard_map/reduce_scatter | solution.py:300
  1474.2 89.6 %reduce-scatter.19.cloned.1.call-done = bf16[512,2048]{1,0:T(8,128)(2,1)} async-done(((bf16[2048,2048]{1,0:T(8,128)(2,1)}), bf16[512,2048]{1,0:T(8,128)(2,1)}) %reduce-scatter.19.cloned.1.call-update) | async-done | bytes 2097168 | tf_op jit(solution)/shard_map/reduce_scatter | solution.py:306
  1563.8 291.6 %reduce-scatter.23.cloned.1.call-done = bf16[2048,2048]{1,0:T(8,128)(2,1)} async-done(((bf16[2048,8192]{1,0:T(8,128)(2,1)}), bf16[2048,2048]{1,0:T(8,128)(2,1)}) %reduce-scatter.23.cloned.1.call-update) | async-done | bytes 8388624 | tf_op jit(solution)/shard_map/reduce_scatter | solution.py:192
  1855.5 291.9 %reduce-scatter.29.cloned.1.call-done = bf16[2048,2048]{1,0:T(8,128)(2,1)} async-done(((bf16[8192,2048]{1,0:T(8,128)(2,1)}), bf16[2048,2048]{1,0:T(8,128)(2,1)}) %reduce-scatter.29.cloned.1.call-update) | async-done | bytes 8388624
  2166.3 18.1 fusion.52
  2214.5 30.3 %all-reduce.10 = (bf16[512]{0:T(512)(128)(2,1)S(1)}, bf16[512]{0:T(512)(128)(2,1)S(1)}, bf16[512]{0:T(512)(128)(2,1)S(1)}, bf16[512]{0:T(512)(128)(2,1)S(1)}, bf...) all-reduce(bf16[512]{0:T(512)(128)(2,1)S(1)} %dynamic-slice.1, ...), channel_id=1, replica_groups=mesh['replica'=8,'group'=4] {'replica'}, use_global_device_ids=true, to_apply=%region_19.20 | all-reduce | flops 6144 | bytes 24576 | tf_op jit(solution)/shard_map/psum | solution.py:329
  2251.3 49.1 %all-gather.35.cloned.1.call-done = bf16[4096,2048]{1,0:T(8,128)(2,1)} async-done(((bf16[512,2048]{1,0:T(8,128)(2,1)}), bf16[4096,2048]{1,0:T(8,128)(2,1)}) %all-gather.35.cloned.1.call-update) | async-done | bytes 16777232 | tf_op jit(solution)/shard_map/all_gather | solution.py:13
  2312.8 442.9 %all-reduce.15.cloned.1.call-done = (bf16[512,2048]{1,0:T(8,128)(2,1)}, bf16[512,2048]{1,0:T(8,128)(2,1)}, bf16[512,2048]{1,0:T(8,128)(2,1)}, bf16[2048,2048]{1,0:T(8,128)(2,1)}, bf16[2048,2048]{1,0:T(8,128)(2,1)}) async-done(((bf16[512,2048]{1,0:T(8,128)(2,1)}, bf16[512,2048]{1,0:T(8,128)(2,1)}, bf16[512,2048]{1,0:T(8,128)(2,1)}, bf16[2048,2048]{1,0:T(8,128)(2,1)}, bf16[2048,2048]{1,0:T(8,128)(2,1)}), ...) | async-done | bytes 23068688 | tf_op jit(solution)/shard_map/psum | solution.py:333
  (294 shorter events, 342.9 us)
Async XLA Ops:
  7.2 19.9 copy-start.23
  7.2 27.1 copy-start
  7.2 93.1 %all-gather.19.cloned.1.call-start = ((), (), s32[]{:S(2)}) async-start(), calls=%async_computation.8 | async-start | bytes 10485760 | tf_op jit(solution)/shard_map/all_gather | solution.py:121
  8.0 181.9 %all-gather.25.cloned.1.call-start = ((), (), s32[]{:S(2)}) async-start(), calls=%async_computation.11 | async-start | bytes 10485760 | tf_op jit(solution)/shard_map/all_gather | solution.py:120
  8.7 270.9 %all-gather.23.cloned.1.call-start = ((), (), s32[]{:S(2)}) async-start(), calls=%async_computation.10 | async-start | bytes 10485760 | tf_op jit(solution)/shard_map/all_gather | solution.py:119
  9.4 307.7 %all-gather.21.cloned.1.call-start = ((), (), s32[]{:S(2)}) async-start(), calls=%async_computation.9 | async-start | bytes 2621440 | tf_op jit(solution)/shard_map/all_gather | solution.py:139
  105.9 248.9 %all-gather.27.cloned.1.call-start = ((), (), s32[]{:S(2)}) async-start(), calls=%async_computation.12 | async-start | bytes 2621440 | tf_op jit(solution)/shard_map/all_gather | solution.py:138
  195.4 248.8 %all-gather.29.cloned.1.call-start = ((), (), s32[]{:S(2)}) async-start(), calls=%async_computation.13 | async-start | bytes 10485760 | tf_op jit(solution)/shard_map/all_gather | solution.py:122
  195.9 547.3 %all-gather.31.cloned.1.call-start = ((), (), s32[]{:S(2)}) async-start(), calls=%async_computation.14 | async-start | bytes 41943040 | tf_op jit(solution)/shard_map/all_gather | solution.py:165
  196.7 25.1 copy-start.26
  196.7 32.2 %copy-start.27 = (bf16[512]{0:T(512)(128)(2,1)S(1)}, bf16[512]{0:T(512)(128)(2,1)}, u32[]{:S(2)}) copy-start(bf16[512]{0:T(512)(128)(2,1)} %param.35) | copy-start | bytes 3076
  196.7 40.3 %copy-start.29 = (s32[128]{0:T(128)S(1)}, s32[128]{0:T(128)}, u32[]{:S(2)}) copy-start(s32[128]{0:T(128)} %param.25) | copy-start | bytes 1540
  196.8 845.6 %all-gather.33.cloned.1.call-start = ((), (), s32[]{:S(2)}) async-start(), calls=%async_computation.15 | async-start | bytes 41943040 | tf_op jit(solution)/shard_map/all_gather | solution.py:167
  197.5 968.0 %reduce-scatter.25.cloned.1.call-start = ((), (), s32[]{:S(2)}) async-start(), calls=%async_computation.22 | async-start | bytes 2621440
  1130.2 74.2 %reduce-scatter.27.cloned.1.call-start = ((), (), s32[]{:S(2)}) async-start(), calls=%async_computation.23 | async-start | bytes 2621440
  1134.2 160.3 %reduce-scatter.15.cloned.1.call-start = ((), (), s32[]{:S(2)}) async-start(), calls=%async_computation.16 | async-start | bytes 10485760 | tf_op jit(solution)/shard_map/reduce_scatter | solution.py:294
  1140.2 244.0 %reduce-scatter.21.cloned.1.call-start = ((), (), s32[]{:S(2)}) async-start(), calls=%async_computation.19 | async-start | bytes 10485760 | tf_op jit(solution)/shard_map/reduce_scatter | solution.py:312
  1146.9 327.3 %reduce-scatter.17.cloned.1.call-start = ((), (), s32[]{:S(2)}) async-start(), calls=%async_computation.17 | async-start | bytes 10485760 | tf_op jit(solution)/shard_map/reduce_scatter | solution.py:300
  1172.5 391.4 %reduce-scatter.19.cloned.1.call-start = ((), (), s32[]{:S(2)}) async-start(), calls=%async_computation.18 | async-start | bytes 10485760 | tf_op jit(solution)/shard_map/reduce_scatter | solution.py:306
  1211.2 644.3 %reduce-scatter.23.cloned.1.call-start = ((), (), s32[]{:S(2)}) async-start(), calls=%async_computation.20 | async-start | bytes 41943040 | tf_op jit(solution)/shard_map/reduce_scatter | solution.py:192
  1228.1 919.3 %reduce-scatter.29.cloned.1.call-start = ((), (), s32[]{:S(2)}) async-start(), calls=%async_computation.24 | async-start | bytes 41943040
  1245.7 1054.8 %all-gather.35.cloned.1.call-start = ((), (), s32[]{:S(2)}) async-start(), calls=%async_computation.21 | async-start | bytes 18874368 | tf_op jit(solution)/shard_map/all_gather | solution.py:13
  1294.5 1461.2 %all-reduce.15.cloned.1.call-start = ((), (), s32[]{:S(2)}) async-start(), calls=%async_computation.25 | async-start | bytes 46137344 | tf_op jit(solution)/shard_map/psum | solution.py:333
  2191.1 59.0 %copy-start.12 = (f32[128,2048]{1,0:T(8,128)S(1)}, f32[128,2048]{1,0:T(8,128)}, u32[]{:S(2)}) copy-start(f32[128,2048]{1,0:T(8,128)} %get-tuple-element.223) | copy-start | bytes 3145732
  (49 other events, 140.6 us)
Sparse Core Ops, SparseCore 0:
  9.9 90.3 all-gather.18
  102.2 87.5 all-gather.24
  191.7 87.8 all-gather.22
  281.8 35.3 all-gather.20
  319.5 35.2 all-gather.26
  356.5 87.5 all-gather.28
  446.0 297.2 all-gather.30
  745.1 297.2 all-gather.32
  1130.3 35.1 reduce-scatter.24
  1169.2 35.1 reduce-scatter.26
  1208.1 86.3 reduce-scatter.14
  1297.7 86.3 reduce-scatter.20
  1387.8 86.3 reduce-scatter.16
  1477.4 86.3 reduce-scatter.18
  1566.8 288.6 reduce-scatter.22
  1858.7 288.6 reduce-scatter.28
  2148.8 151.6 all-gather.34
  2303.4 452.2 all-reduce.14
